TPU v7x, 32 devices: a whole 2x2x4 slice. The times are simulated.
32 devices in a mesh: leaf: 4 (over x, core), blk: 8 (over z, y).
Axes of the slice: x: 2, y: 2, z: 4, core: 2. Of those that a mesh axis runs over, the one named last changes fastest.
Arguments:
- right_side: float32 [4, 8, 448, 128], P('leaf', 'blk'), may hold values from -6 to 6
- inverse_blocks: bfloat16 [4, 8, 448, 2048], P('leaf', 'blk'), may hold values from -0.125 to 0.125
- coupling: bfloat16 [4, 8, 640, 1024], P('leaf', 'blk'), may hold values from -0.0625 to 0.0625
- update_rows: int32 [10, 1024], replicated, may hold values from 0 to 2047, as said below
Outputs:
- solution: float32 [4, 8, 448, 128], P('leaf', 'blk')
Inputs may be any that keep to these rules, and one draw needn't show every extreme that they name: `update_rows`: the 1024 entries of each row are distinct.
All inputs are finite; a program needn't handle non-finite values.
Results may differ from a plain program's by a relative error of at most 0.0075.
Values may be sent and summed in bfloat16 or wider, within the bound.
No kernel may reach another device: no remote copies, remote signals or barrier semaphores. Data moves between devices by JAX's collectives and lax.ppermute only.
A program may use at most 64 MiB of HBM per device.

v0:
```python
import jax
import jax.numpy as jnp
from jax import lax
from jax.sharding import PartitionSpec as P


def from_partner(shard, axis, distance):
    return lax.ppermute(shard, axis, [(i, i ^ 1 << distance) for i in range(lax.axis_size(axis))])


def group_total(partial_value, level_no, leaf_id, want_full):
    members = partial_value.shape[0]
    member = leaf_id & members - 1
    full_rows = None
    summed = lax.psum_scatter(partial_value, "blk", scatter_dimension=1, tiled=True)
    for bit_no in range(level_no):
        summed = summed + from_partner(summed, "leaf", bit_no)
    own_rows = lax.dynamic_index_in_dim(summed, member, 0, keepdims=False)[0]
    if want_full:
        full_rows = lax.all_gather(summed.astype(jnp.bfloat16), "blk", axis=1, tiled=True)
    if full_rows is not None:
        full_rows = full_rows.reshape(-1, full_rows.shape[-1])
    return (own_rows, full_rows)


def local(right_side, inverse_blocks, coupling, update_rows):
    leaves = lax.axis_size("leaf")
    blocks = lax.axis_size("blk")
    tree_depth = leaves.bit_length() - 1
    leaf_id = lax.axis_index("leaf")
    blk_id = lax.axis_index("blk")
    node_width = inverse_blocks.shape[-1]
    load_cases = right_side.shape[-1]
    local_rhs = right_side[0, 0]
    local_inverse = inverse_blocks[0, 0]
    local_coupling = coupling[0, 0]
    row_counts = [node_width // (blocks << level_no) for level_no in range(tree_depth + 1)]
    row_starts = [sum(row_counts[:level_no]) for level_no in range(tree_depth + 1)]
    coupling_starts = {}
    cursor = 0
    for level_no in range(tree_depth):
        for ancestor in range(level_no + 1, tree_depth + 1):
            coupling_starts[level_no, ancestor] = cursor
            cursor += row_counts[level_no]
    pair_bases = []
    cursor = 0
    for level_no in range(tree_depth + 1):
        pair_bases.append(cursor)
        cursor += (leaves >> level_no) * (tree_depth - level_no)

    def coupling_block(level_no, ancestor):
        coup_start = coupling_starts[level_no, ancestor]
        return local_coupling[coup_start : coup_start + row_counts[level_no]]

    def row_list(level_no, ancestor):
        node_id = leaf_id >> level_no
        pair_row = (
            pair_bases[level_no] + node_id * (tree_depth - level_no) + (ancestor - level_no - 1)
        )
        return lax.dynamic_index_in_dim(update_rows, pair_row, 0, keepdims=False)

    pending = {}
    y_levels = []
    for level_no in range(tree_depth + 1):
        members = 1 << level_no
        row_count = row_counts[level_no]
        row_start = row_starts[level_no]
        member = leaf_id & members - 1
        if level_no == 0:
            residual = lax.all_gather(
                local_rhs[row_start : row_start + row_count].astype(jnp.bfloat16),
                "blk",
                axis=0,
                tiled=True,
            )
        else:
            buffer = pending.get(level_no, jnp.zeros((node_width, load_cases), jnp.float32))
            slot_start = (member * blocks + blk_id) * row_count
            current = lax.dynamic_slice_in_dim(buffer, slot_start, row_count, 0)
            buffer = lax.dynamic_update_slice_in_dim(
                buffer, current + local_rhs[row_start : row_start + row_count], slot_start, 0
            )
            unused_rows, residual = group_total(
                buffer.reshape(members, blocks, row_count, load_cases), level_no, leaf_id, True
            )
        inverse_rows = local_inverse[row_start : row_start + row_count]
        y_rows = jnp.dot(inverse_rows, residual, preferred_element_type=jnp.float32)
        y_levels.append(y_rows)
        y_round = y_rows.astype(jnp.bfloat16)
        for ancestor in range(level_no + 1, tree_depth + 1):
            contrib = lax.dot_general(
                coupling_block(level_no, ancestor),
                y_round,
                (((0,), (0,)), ((), ())),
                preferred_element_type=jnp.float32,
            )
            summed = pending.get(ancestor, jnp.zeros((node_width, load_cases), jnp.float32))
            pending[ancestor] = summed.at[row_list(level_no, ancestor)].add(-contrib)
    solved = {}
    outputs = [None] * (tree_depth + 1)
    for level_no in range(tree_depth, -1, -1):
        members = 1 << level_no
        row_count = row_counts[level_no]
        row_start = row_starts[level_no]
        z_rows = y_levels[level_no]
        for ancestor in range(level_no + 1, tree_depth + 1):
            picked = jnp.take(solved[ancestor], row_list(level_no, ancestor), axis=0)
            z_rows = z_rows - jnp.dot(
                coupling_block(level_no, ancestor), picked, preferred_element_type=jnp.float32
            )
        inverse_rows = local_inverse[row_start : row_start + row_count]
        partial_value = lax.dot_general(
            inverse_rows,
            z_rows.astype(jnp.bfloat16),
            (((0,), (0,)), ((), ())),
            preferred_element_type=jnp.float32,
        )
        own_rows, full_rows = group_total(
            partial_value.reshape(members, blocks, row_count, load_cases),
            level_no,
            leaf_id,
            level_no > 0,
        )
        outputs[level_no] = own_rows
        if level_no > 0:
            solved[level_no] = full_rows
    return jnp.concatenate(outputs, 0)[None, None]


def solution(mesh):
    in_specs = (
        P("leaf", "blk", None, None),
        P("leaf", "blk", None, None),
        P("leaf", "blk", None, None),
        P(),
    )
    out_specs = P("leaf", "blk", None, None)
    return jax.shard_map(local, mesh=mesh, in_specs=in_specs, out_specs=out_specs, check_vma=False)
```

profile of v0, /device:TPU:0, one launch (start us, length us, event | category | flops | bytes accessed | tf_op | source)
XLA Modules:
  0.0 612.2 jit_solution(16145240339841454955)
XLA Ops:
  6.5 1.0 slice.135
  7.6 33.0 %all-gather = bf16[1,1,2048,128]{3,2,1,0:T(8,128)(2,1)S(1)} all-gather(bf16[1,1,256,128]{3,2,1,0:T(8,128)(2,1)S(1)} %slice.135), channel_id=2, replica_groups=mesh['leaf'=4,'blk'=8] {'blk'}, dimensions={2}, use_global_device_ids=true | all-gather | bytes 589824 | tf_op jit(solution)/shard_map/all_gather | solution.py:70
  40.6 1.6 fusion.8
  42.2 0.3 fusion.2
  42.5 0.2 copy.20
  42.7 0.0 copy-start.8
  42.7 1.4 compare_select_fusion.2
  44.2 6.3 %scatter_custom_fusion = f32[2048,128]{1,0:T(8,128)S(1)} fusion(s32[1024]{0:T(1024)S(1)} %bitcast.138, f32[1024,128]{1,0:T(8,128)S(1)} %copy.20, f32[]{:T(128)} %constant.56.clone.1), kind=kCustom, calls=%fused_computation.38 | custom fusion | flops 131072 | bytes 1048580 | tf_op jit(solution)/shard_map/scatter-add | solution.py:98
  50.4 0.9 fusion.57
  51.3 1.0 copy-done.1
  52.3 0.0 all-reduce.7.cloned.1.call-update
  52.3 0.0 all-reduce.9.cloned.1.call-start
  52.4 0.7 dynamic-slice
  53.1 78.9 %all-reduce.7.cloned.1.call-done = f32[2,8,128,128]{3,2,1,0:T(8,128)} async-done(((f32[2,8,128,128]{3,2,1,0:T(8,128)}), f32[2,8,128,128]{3,2,1,0:T(8,128)}) %all-reduce.7.cloned.1.call-update) | async-done | bytes 1048592
  132.0 2.2 constant_dynamic-slice_fusion.5
  134.2 0.3 fusion.1
  134.5 0.2 copy.21
  134.7 6.5 %scatter_custom_fusion.1 = f32[2048,128]{1,0:T(8,128)S(1)} fusion(s32[1024]{0:T(1024)} %bitcast.137, f32[1024,128]{1,0:T(8,128)S(1)} %copy.21, f32[]{:T(128)} %constant.56.clone.1), kind=kCustom, calls=%fused_computation.36 | custom fusion | flops 131072 | bytes 1049088 | tf_op jit(solution)/shard_map/scatter-add | solution.py:98
  141.3 1.6 add_convert_fusion.1
  142.9 31.4 %all_gather.16 = bf16[2,8,128,128]{3,2,1,0:T(8,128)(2,1)S(1)} all-gather(bf16[2,1,128,128]{3,2,1,0:T(8,128)(2,1)S(1)} %add_convert_fusion.1), channel_id=1, replica_groups=mesh['leaf'=4,'blk'=8] {'blk'}, dimensions={1}, use_global_device_ids=true | all-gather | bytes 589824 | tf_op jit(solution)/shard_map/all_gather | solution.py:20
  174.3 0.3 fusion.16
  174.6 2.0 fusion
  176.6 1.2 copy.22
  177.8 6.4 %scatter_fusion = f32[2048,128]{1,0:T(8,128)S(1)} fusion(f32[2048,128]{1,0:T(8,128)S(1)} %scatter_custom_fusion.1, s32[1024]{0:T(1024)S(1)} %bitcast.136, f32[1024,128]{1,0:T(8,128)S(1)} %copy.22), kind=kCustom, calls=%fused_computation.5 | custom fusion | flops 131072 | bytes 1576960 | tf_op jit(solution)/shard_map/scatter-add | solution.py:98
  184.3 0.8 fusion.58
  185.0 1.0 copy-done
  186.0 0.0 all-reduce.9.cloned.1.call-update
  186.1 0.0 all-reduce.11.cloned.1.call-start
  186.1 77.9 %all-reduce.9.cloned.1.call-done = f32[4,8,64,128]{3,2,1,0:T(8,128)} async-done(((f32[4,8,64,128]{3,2,1,0:T(8,128)}), f32[4,8,64,128]{3,2,1,0:T(8,128)}) %all-reduce.9.cloned.1.call-update) | async-done | bytes 1048592
  264.0 1.6 constant_dynamic-slice_fusion.4
  265.6 0.1 collective-permute-start.1
  265.7 1.3 collective-permute-done.1
  267.0 1.6 fusion.75
  268.6 1.5 collective-permute-start.2
  270.1 4.1 collective-permute-done.2
  274.2 31.3 %all_gather.17 = bf16[4,8,64,128]{3,2,1,0:T(8,128)(2,1)S(1)} all-gather(bf16[4,1,64,128]{3,2,1,0:T(8,128)(2,1)S(1)} %add_convert_fusion), channel_id=1, replica_groups=mesh['leaf'=4,'blk'=8] {'blk'}, dimensions={1}, use_global_device_ids=true | all-gather | bytes 589824 | tf_op jit(solution)/shard_map/all_gather | solution.py:20
  305.5 0.5 convolution_bitcast_fusion.1
  306.0 1.4 copy.23
  307.4 0.0 all-reduce.11.cloned.1.call-update
  307.4 0.0 reduce-scatter.12.cloned.1.call-start
  307.5 78.2 %all-reduce.11.cloned.1.call-done = f32[4,8,64,128]{3,2,1,0:T(8,128)} async-done(((f32[4,8,64,128]{3,2,1,0:T(8,128)}), f32[4,8,64,128]{3,2,1,0:T(8,128)}) %all-reduce.11.cloned.1.call-update) | async-done | bytes 1048592
  385.6 1.6 constant_dynamic-slice_fusion.3
  387.2 0.1 collective-permute-start.3
  387.3 1.3 collective-permute-done.3
  388.6 1.6 fusion.74
  390.2 1.5 collective-permute-start.4
  391.8 4.1 collective-permute-done.4
  395.9 31.3 %all_gather.18 = bf16[4,8,64,128]{3,2,1,0:T(8,128)(2,1)S(1)} all-gather(bf16[4,1,64,128]{3,2,1,0:T(8,128)(2,1)S(1)} %get-tuple-element.8), channel_id=1, replica_groups=mesh['leaf'=4,'blk'=8] {'blk'}, dimensions={1}, use_global_device_ids=true | all-gather | bytes 589824 | tf_op jit(solution)/shard_map/all_gather | solution.py:20
  427.1 3.2 gather_fusion
  430.4 2.0 convolution_bitcast_fusion.2
  432.3 0.2 copy.38
  432.5 1.4 copy.24
  433.9 0.0 reduce-scatter.12.cloned.1.call-update
  434.0 0.0 reduce-scatter.14.cloned.1.call-start
  434.0 64.1 %reduce-scatter.12.cloned.1.call-done = f32[2,1,128,128]{3,2,0,1:T(8,128)} async-done(((f32[2,8,128,128]{3,2,0,1:T(8,128)}), f32[2,1,128,128]{3,2,0,1:T(8,128)}) %reduce-scatter.12.cloned.1.call-update) | async-done | bytes 131088 | tf_op jit(solution)/shard_map/reduce_scatter | solution.py:15
  498.1 3.2 gather_fusion.2
  501.4 31.5 %all_gather.19 = bf16[2,8,128,128]{3,2,0,1:T(8,128)(2,1)S(1)} all-gather(bf16[2,1,128,128]{3,2,0,1:T(8,128)(2,1)S(1)} %get-tuple-element.6), channel_id=1, replica_groups=mesh['leaf'=4,'blk'=8] {'blk'}, dimensions={1}, use_global_device_ids=true | all-gather | bytes 589824 | tf_op jit(solution)/shard_map/all_gather | solution.py:20
  532.9 3.2 gather_fusion.1
  536.1 1.5 fusion.4
  537.6 1.8 convolution_bitcast_fusion
  539.4 1.3 copy.31
  540.7 0.0 reduce-scatter.14.cloned.1.call-update
  540.8 63.3 %reduce-scatter.14.cloned.1.call-done = f32[1,1,256,128]{3,2,1,0:T(8,128)} async-done(((f32[1,8,256,128]{3,2,1,0:T(8,128)}), f32[1,1,256,128]{3,2,1,0:T(8,128)}) %reduce-scatter.14.cloned.1.call-update) | async-done | bytes 131088 | tf_op jit(solution)/shard_map/reduce_scatter | solution.py:15
  604.1 1.6 maximum_bitcast_fusion
  (31 shorter events, 0.2 us)
Async XLA Ops:
  6.5 125.5 %all-reduce.7.cloned.1.call-start = ((), (), s32[]{:S(2)}) async-start(), calls=%async_computation.4 | async-start | bytes 2097152
  6.5 35.7 %copy-start.4 = (bf16[1,1,640,1024]{3,2,1,0:T(8,128)(2,1)S(1)}, bf16[1,1,640,1024]{3,2,1,0:T(8,128)(2,1)}, u32[]{:S(2)}) copy-start(bf16[1,1,640,1024]{3,2,1,0:T(8,128)(2,1)} %param.8) | copy-start | bytes 3932164
  42.2 92.0 %copy-start.5 = (f32[256,128]{1,0:T(8,128)}, f32[256,128]{1,0:T(8,128)S(1)}, u32[]{:S(2)}) copy-start(f32[256,128]{1,0:T(8,128)S(1)} %fusion.8) | copy-start | bytes 393220
  42.7 9.7 %copy-start.8 = (u32[32]{0:T(128)S(1)}, u32[32]{0:T(128)}, u32[]{:S(2)}) copy-start(u32[32]{0:T(128)} %constant.76) | copy-start | bytes 388
  51.3 1.0 copy-start.1
  52.3 211.6 %all-reduce.9.cloned.1.call-start = ((), (), s32[]{:S(2)}) async-start(), calls=%async_computation.5 | async-start | bytes 2097152
  134.2 7.0 %collective-permute-start = (f32[2,1,128,128]{3,2,1,0:T(8,128)}, f32[2,1,128,128]{3,2,1,0:T(8,128)S(1)}, u32[]{:S(2)}, u32[]{:S(2)}) collective-permute-start(f32[2,1,128,128]{3,2,1,0:T(8,128)} %constant_dynamic-slice_fusion.5), channel_id=1, source_target_pairs={{0,8},{8,0},{16,24},{24,16},{1,9},{9,1},{17,25},{25,17},{2,10},{10... | collective-permute-start | bytes 393224 | tf_op jit(solution)/shard_map/ppermute | solution.py:8
  134.5 39.8 %copy-start.2 = (bf16[1,1,448,2048]{3,2,1,0:T(8,128)(2,1)S(1)}, bf16[1,1,448,2048]{3,2,1,0:T(8,128)(2,1)}, u32[]{:S(2)}) copy-start(bf16[1,1,448,2048]{3,2,1,0:T(8,128)(2,1)} %param.7) | copy-start | bytes 5505028
  185.0 1.0 copy-start
  186.1 199.6 %all-reduce.11.cloned.1.call-start = ((), (), s32[]{:S(2)}) async-start(), calls=%async_computation.6 | async-start | bytes 2097152
  265.6 1.4 collective-permute-start.1
  268.6 5.6 collective-permute-start.2
  307.4 190.7 %reduce-scatter.12.cloned.1.call-start = ((), (), s32[]{:S(2)}) async-start(), calls=%async_computation.2 | async-start | bytes 1179648 | tf_op jit(solution)/shard_map/reduce_scatter | solution.py:15
  387.2 1.4 collective-permute-start.3
  390.2 5.6 collective-permute-start.4
  434.0 170.1 %reduce-scatter.14.cloned.1.call-start = ((), (), s32[]{:S(2)}) async-start(), calls=%async_computation.3 | async-start | bytes 1179648 | tf_op jit(solution)/shard_map/reduce_scatter | solution.py:15
  498.1 3.2 copy-start.7
  498.1 3.2 collective-permute-start.5
  532.9 3.2 copy-start.6
  532.9 4.7 copy-start.3
Sparse Core Ops, SparseCore 0:
  52.5 79.4 all-reduce.6
  186.2 77.7 all-reduce.8
  307.5 78.0 all-reduce.10
  434.1 63.9 reduce-scatter.11
  540.9 63.1 reduce-scatter.13
where the time goes:
time: 613 us; the launch traced here: 612 us
  waiting for transfers between devices  373 us (61%)
  blocking collectives  158 us (26%)
  other arithmetic  28.8 us (5%)
  local copies, waits for them, and re-layouts  24.7 us (4%)
  between operations  13.5 us (2%)
  matrix products  10.2 us (2%)
    unnamed x8, waiting for transfers between devices  235 us
    reduce_scatter x2, waiting for transfers between devices, group_total(): lax.psum_scatter(partial_value, 'blk', scatter_dimension=1, tiled=True)  127 us
    all_gather x4, blocking collectives, group_total(): lax.all_gather(summed.astype(jnp.bfloat16), 'blk', axis=1, tiled=True)  125 us
    all_gather x1, blocking collectives, local(): lax.all_gather(local_rhs[row_start:row_start + row_count].astype(jnp.bflo...  33 us
    scatter-add x3, other arithmetic, local(): pending[ancestor] = summed.at[row_list(level_no, ancestor)].add(-contrib)  19.2 us
  transfers between devices with their start and end apart: 11, of which 9 were waited for; matrix products, arithmetic and copies ran while one was open for 2% of the time, Pallas kernels for 0%

commit v1 on v0

--- a/solution.py
+++ b/solution.py
@@ -2,6 +2,13 @@
 import jax.numpy as jnp
 from jax import lax
 from jax.sharding import PartitionSpec as P
+
+
+def create_pages(frame_in):
+    local_out = jnp.concatenate(
+        lax.all_to_all(jnp.stack([frame_in] * lax.axis_size("blk"), 0), "blk", 0, 0), 1
+    )
+    return local_out
 
 
 def from_partner(shard, axis, distance):
@@ -17,7 +24,7 @@
         summed = summed + from_partner(summed, "leaf", bit_no)
     own_rows = lax.dynamic_index_in_dim(summed, member, 0, keepdims=False)[0]
     if want_full:
-        full_rows = lax.all_gather(summed.astype(jnp.bfloat16), "blk", axis=1, tiled=True)
+        full_rows = create_pages(summed.astype(jnp.bfloat16))
     if full_rows is not None:
         full_rows = full_rows.reshape(-1, full_rows.shape[-1])
     return (own_rows, full_rows)

time: 613 us -> 554 us (0.904)
  blocking collectives: 158 us -> 51 us
  waiting for transfers between devices: 373 us -> 406 us
  starting transfers between devices: 3.38 us -> 15.5 us
    all_gather x4 -> x0, blocking collectives: 125 us -> none  [group_total(): lax.all_gather(summed.astype(jnp.bfloat16), 'blk', axis=1, tiled=True)]
    all_to_all x0 -> x3, waiting for transfers between devices: none -> 32.2 us  [create_pages(): lax.all_to_all(jnp.stack([frame_in] * lax.axis_size('blk'), 0), 'blk', 0, 0)]
    all_to_all x0 -> x1, blocking collectives: none -> 17.9 us  [create_pages(): lax.all_to_all(jnp.stack([frame_in] * lax.axis_size('blk'), 0), 'blk', 0, 0)]
    all_to_all x0 -> x3, starting transfers between devices: none -> 12 us  [create_pages(): lax.all_to_all(jnp.stack([frame_in] * lax.axis_size('blk'), 0), 'blk', 0, 0)]
  transfers between devices with their start and end apart: 11 -> 14, of which waited for: 9 -> 14; matrix products, arithmetic and copies ran while one was open for 2% -> 2% of each run, Pallas kernels for 0% -> 0%
where the time goes in v1:
time: 554 us; the launch traced here: 553 us
  waiting for transfers between devices  406 us (73%)
  blocking collectives  51 us (9%)
  other arithmetic  29.2 us (5%)
  local copies, waits for them, and re-layouts  27.5 us (5%)
  starting transfers between devices  15.5 us (3%)
  between operations  13.5 us (2%)
  matrix products  10.2 us (2%)
    unnamed x8, waiting for transfers between devices  234 us
    reduce_scatter x2, waiting for transfers between devices, group_total(): lax.psum_scatter(partial_value, 'blk', scatter_dimension=1, tiled=True)  127 us
    all_gather x1, blocking collectives, local(): lax.all_gather(local_rhs[row_start:row_start + row_count].astype(jnp.bflo...  33 us
    all_to_all x3, waiting for transfers between devices, create_pages(): lax.all_to_all(jnp.stack([frame_in] * lax.axis_size('blk'), 0), 'blk', 0, 0)  32.2 us
    scatter-add x3, other arithmetic, local(): pending[ancestor] = summed.at[row_list(level_no, ancestor)].add(-contrib)  19.5 us
    all_to_all x1, blocking collectives, create_pages(): lax.all_to_all(jnp.stack([frame_in] * lax.axis_size('blk'), 0), 'blk', 0, 0)  17.9 us
    ppermute x6, waiting for transfers between devices, from_partner(): lax.ppermute(shard, axis, [(i, i ^ 1 << distance) for i in range(lax.axis...  13.7 us
    all_to_all x3, starting transfers between devices, create_pages(): lax.all_to_all(jnp.stack([frame_in] * lax.axis_size('blk'), 0), 'blk', 0, 0)  12 us
  transfers between devices with their start and end apart: 14, of which 14 were waited for; matrix products, arithmetic and copies ran while one was open for 2% of the time, Pallas kernels for 0%

profile of v1, /device:TPU:0, one launch (start us, length us, event | category | flops | bytes accessed | tf_op | source)
XLA Modules:
  0.0 553.4 jit_solution(11021629262132525457)
XLA Ops:
  6.5 1.0 slice.135
  7.6 33.0 %all-gather = bf16[1,1,2048,128]{3,2,1,0:T(8,128)(2,1)S(1)} all-gather(bf16[1,1,256,128]{3,2,1,0:T(8,128)(2,1)S(1)} %slice.135), channel_id=2, replica_groups=mesh['leaf'=4,'blk'=8] {'blk'}, dimensions={2}, use_global_device_ids=true | all-gather | bytes 589824 | tf_op jit(solution)/shard_map/all_gather | solution.py:77
  40.6 1.6 fusion.8
  42.2 0.3 fusion.2
  42.5 0.2 copy.19
  42.7 0.9 compare_select_fusion.2
  43.6 6.3 %scatter_custom_fusion = f32[2048,128]{1,0:T(8,128)S(1)} fusion(s32[1024]{0:T(1024)S(1)} %bitcast.159, f32[1024,128]{1,0:T(8,128)S(1)} %copy.19, f32[]{:T(128)} %constant.56.clone.1), kind=kCustom, calls=%fused_computation.38 | custom fusion | flops 131072 | bytes 1048580 | tf_op jit(solution)/shard_map/scatter-add | solution.py:105
  49.9 0.9 fusion.59
  50.8 1.0 copy-done.1
  51.8 0.6 dynamic-slice
  52.4 79.0 %all-reduce.7.cloned.1.call-done = f32[2,8,128,128]{3,2,1,0:T(8,128)} async-done(((f32[2,8,128,128]{3,2,1,0:T(8,128)}), f32[2,8,128,128]{3,2,1,0:T(8,128)}) %all-reduce.7.cloned.1.call-update) | async-done | bytes 1048592
  131.4 1.5 constant_dynamic-slice_fusion.4
  132.9 0.1 collective-permute-start
  133.0 1.3 collective-permute-done
  134.4 1.5 fusion.57
  135.9 0.9 stack.8
  136.8 4.2 all-to-all-start
  141.1 0.3 fusion.1
  141.3 1.0 copy.21
  142.3 6.8 %scatter_custom_fusion.1 = f32[2048,128]{1,0:T(8,128)S(1)} fusion(s32[1024]{0:T(1024)S(1)} %bitcast.158, f32[1024,128]{1,0:T(8,128)} %copy.21, f32[]{:T(128)} %constant.56.clone.1), kind=kCustom, calls=%fused_computation.36 | custom fusion | flops 131072 | bytes 1049088 | tf_op jit(solution)/shard_map/scatter-add | solution.py:105
  149.1 6.7 %all-to-all-done = bf16[8,2,1,128,128]{4,3,1,2,0:T(8,128)(2,1)S(1)} async-done(((bf16[8,2,1,128,128]{4,3,1,2,0:T(8,128)(2,1)}), bf16[8,2,1,128,128]{4,3,1,2,0:T(8,128)(2,1)S(1)}, u32[]{:S(2)}, u32[]{:S(2)}) %all-to-all-start) | async-done | bytes 524320 | tf_op jit(solution)/shard_map/all_to_all | solution.py:9
  155.9 0.3 fusion.16
  156.2 2.0 fusion
  158.2 1.2 copy.22
  159.4 6.4 %scatter_fusion = f32[2048,128]{1,0:T(8,128)S(1)} fusion(f32[2048,128]{1,0:T(8,128)S(1)} %scatter_custom_fusion.1, s32[1024]{0:T(1024)S(1)} %bitcast.157, f32[1024,128]{1,0:T(8,128)S(1)} %copy.22), kind=kCustom, calls=%fused_computation.5 | custom fusion | flops 131072 | bytes 1576960 | tf_op jit(solution)/shard_map/scatter-add | solution.py:105
  165.9 0.8 fusion.60
  166.6 1.0 copy-done
  167.7 77.4 %all-reduce.9.cloned.1.call-done = f32[4,8,64,128]{3,2,1,0:T(8,128)} async-done(((f32[4,8,64,128]{3,2,1,0:T(8,128)}), f32[4,8,64,128]{3,2,1,0:T(8,128)}) %all-reduce.9.cloned.1.call-update) | async-done | bytes 1048592
  245.1 1.5 constant_dynamic-slice_fusion.3
  246.7 1.3 collective-permute-done.1
  248.0 1.5 fusion.75
  249.6 1.5 collective-permute-start.2
  251.1 4.1 collective-permute-done.2
  255.2 0.1 stack.9
  255.3 17.9 %all_to_all.20 = bf16[8,4,1,64,128]{4,3,1,2,0:T(8,128)(2,1)S(1)} all-to-all(bf16[8,4,1,64,128]{4,3,1,2,0:T(8,128)(2,1)S(1)} %stack.9), channel_id=1, replica_groups=mesh['leaf'=4,'blk'=8] {'blk'}, dimensions={0} | all-to-all | bytes 1048576 | tf_op jit(solution)/shard_map/all_to_all | solution.py:9
  273.3 0.5 convolution_bitcast_fusion.1
  273.9 1.3 copy.24
  275.2 77.5 %all-reduce.11.cloned.1.call-done = f32[4,8,64,128]{3,2,1,0:T(8,128)} async-done(((f32[4,8,64,128]{3,2,1,0:T(8,128)}), f32[4,8,64,128]{3,2,1,0:T(8,128)}) %all-reduce.11.cloned.1.call-update) | async-done | bytes 1048592
  352.7 1.5 dynamic-slice_bitcast_fusion
  354.2 0.1 collective-permute-start.3
  354.3 1.3 collective-permute-done.3
  355.6 1.6 fusion.74
  357.2 1.5 collective-permute-start.4
  358.7 4.1 collective-permute-done.4
  362.8 0.9 stack.10
  363.7 4.2 all-to-all-start.2
  368.0 13.9 %all-to-all-done.2 = bf16[8,4,1,64,128]{4,3,1,2,0:T(8,128)(2,1)S(1)} async-done(((bf16[8,4,1,64,128]{4,3,1,2,0:T(8,128)(2,1)}), bf16[8,4,1,64,128]{4,3,1,2,0:T(8,128)(2,1)S(1)}, u32[]{:S(2)}, u32[]{:S(2)}) %all-to-all-start.2) | async-done | bytes 524320 | tf_op jit(solution)/shard_map/all_to_all | solution.py:9
  382.0 3.2 gather_fusion
  385.2 2.0 convolution_bitcast_fusion.2
  387.2 0.2 copy.42
  387.4 1.4 copy.28
  388.8 63.4 %reduce-scatter.12.cloned.1.call-done = f32[2,1,128,128]{3,2,0,1:T(8,128)} async-done(((f32[2,8,128,128]{3,2,0,1:T(8,128)}), f32[2,1,128,128]{3,2,0,1:T(8,128)}) %reduce-scatter.12.cloned.1.call-update) | async-done | bytes 131088 | tf_op jit(solution)/shard_map/reduce_scatter | solution.py:22
  452.2 1.6 collective-permute-done.5
  453.7 0.9 convert_bitcast_fusion
  454.7 0.9 stack.11
  455.5 3.6 all-to-all-start.3
  459.3 3.2 gather_fusion.2
  462.5 11.6 %all-to-all-done.3 = bf16[8,2,1,128,128]{4,3,1,2,0:T(8,128)(2,1)S(1)} async-done(((bf16[8,2,1,128,128]{4,3,1,2,0:T(8,128)(2,1)}), bf16[8,2,1,128,128]{4,3,1,2,0:T(8,128)(2,1)S(1)}, u32[]{:S(2)}, u32[]{:S(2)}) %all-to-all-start.3) | async-done | bytes 524320 | tf_op jit(solution)/shard_map/all_to_all | solution.py:9
  474.1 3.2 gather_fusion.1
  477.3 1.4 fusion.4
  478.8 1.8 convolution_bitcast_fusion
  480.6 1.3 copy.35
  482.0 63.2 %reduce-scatter.14.cloned.1.call-done = f32[1,1,256,128]{3,2,1,0:T(8,128)} async-done(((f32[1,8,256,128]{3,2,1,0:T(8,128)}), f32[1,1,256,128]{3,2,1,0:T(8,128)}) %reduce-scatter.14.cloned.1.call-update) | async-done | bytes 131088 | tf_op jit(solution)/shard_map/reduce_scatter | solution.py:22
  545.2 1.6 maximum_bitcast_fusion
  (38 shorter events, 0.6 us)
Async XLA Ops:
  6.5 124.9 %all-reduce.7.cloned.1.call-start = ((), (), s32[]{:S(2)}) async-start(), calls=%async_computation.8 | async-start | bytes 2097152
  6.5 35.7 %copy-start.4 = (bf16[1,1,640,1024]{3,2,1,0:T(8,128)(2,1)S(1)}, bf16[1,1,640,1024]{3,2,1,0:T(8,128)(2,1)}, u32[]{:S(2)}) copy-start(bf16[1,1,640,1024]{3,2,1,0:T(8,128)(2,1)} %param.8) | copy-start | bytes 3932164
  42.2 98.8 %copy-start.5 = (f32[256,128]{1,0:T(8,128)}, f32[256,128]{1,0:T(8,128)S(1)}, u32[]{:S(2)}) copy-start(f32[256,128]{1,0:T(8,128)S(1)} %fusion.8) | copy-start | bytes 393220
  42.7 9.1 %copy-start.7 = (u32[32]{0:T(128)S(1)}, u32[32]{0:T(128)}, u32[]{:S(2)}) copy-start(u32[32]{0:T(128)} %constant.76) | copy-start | bytes 388
  50.7 1.0 copy-start.1
  132.9 1.4 collective-permute-start
  136.8 19.0 %all-to-all-start = ((bf16[8,2,1,128,128]{4,3,1,2,0:T(8,128)(2,1)}), bf16[8,2,1,128,128]{4,3,1,2,0:T(8,128)(2,1)S(1)}, u32[]{:S(2)}, u32[]{:S(2)}) async-start(bf16[8,2,1,128,128]{4,3,1,2,0:T(8,128)(2,1)} %stack.8), calls=%async_computation | async-start | bytes 1048576 | tf_op jit(solution)/shard_map/all_to_all | solution.py:9
  141.0 104.1 %all-reduce.9.cloned.1.call-start = ((), (), s32[]{:S(2)}) async-start(), calls=%async_computation.9 | async-start | bytes 2097152
  142.3 13.5 %copy-start.2 = (bf16[1,1,448,2048]{3,2,1,0:T(8,128)(2,1)S(1)}, bf16[1,1,448,2048]{3,2,1,0:T(8,128)(2,1)}, u32[]{:S(2)}) copy-start(bf16[1,1,448,2048]{3,2,1,0:T(8,128)(2,1)} %param.7) | copy-start | bytes 5505028
  166.6 1.0 copy-start
  167.6 185.0 %all-reduce.11.cloned.1.call-start = ((), (), s32[]{:S(2)}) async-start(), calls=%async_computation.10 | async-start | bytes 2097152
  246.6 1.4 collective-permute-start.1
  249.6 5.6 %collective-permute-start.2 = (f32[4,1,64,128]{3,2,1,0:T(8,128)S(1)}, f32[4,1,64,128]{3,2,1,0:T(8,128)S(1)}, u32[]{:S(2)}, u32[]{:S(2)}) collective-permute-start(f32[4,1,64,128]{3,2,1,0:T(8,128)S(1)} %fusion.75), channel_id=1, source_target_pairs={{0,16},{8,24},{16,0},{24,8},{1,17},{9,25},{17,1},{25,9},{2,18},{10... | collective-permute-start | bytes 393224 | tf_op jit(solution)/shard_map/ppermute | solution.py:15
  354.2 1.4 collective-permute-start.3
  357.2 5.6 %collective-permute-start.4 = (f32[4,1,64,128]{3,2,0,1:T(8,128)S(1)}, f32[4,1,64,128]{3,2,0,1:T(8,128)S(1)}, u32[]{:S(2)}, u32[]{:S(2)}) collective-permute-start(f32[4,1,64,128]{3,2,0,1:T(8,128)S(1)} %fusion.74), channel_id=1, source_target_pairs={{0,16},{8,24},{16,0},{24,8},{1,17},{9,25},{17,1},{25,9},{2,18},{10... | collective-permute-start | bytes 393224 | tf_op jit(solution)/shard_map/ppermute | solution.py:15
  363.7 18.2 %all-to-all-start.2 = ((bf16[8,4,1,64,128]{4,3,1,2,0:T(8,128)(2,1)}), bf16[8,4,1,64,128]{4,3,1,2,0:T(8,128)(2,1)S(1)}, u32[]{:S(2)}, u32[]{:S(2)}) async-start(bf16[8,4,1,64,128]{4,3,1,2,0:T(8,128)(2,1)} %stack.10), calls=%async_computation.2 | async-start | bytes 1048576 | tf_op jit(solution)/shard_map/all_to_all | solution.py:9
  367.9 84.2 %reduce-scatter.12.cloned.1.call-start = ((), (), s32[]{:S(2)}) async-start(), calls=%async_computation.6 | async-start | bytes 1179648 | tf_op jit(solution)/shard_map/reduce_scatter | solution.py:22
  452.2 1.6 collective-permute-start.5
  455.5 18.5 %all-to-all-start.3 = ((bf16[8,2,1,128,128]{4,3,1,2,0:T(8,128)(2,1)}), bf16[8,2,1,128,128]{4,3,1,2,0:T(8,128)(2,1)S(1)}, u32[]{:S(2)}, u32[]{:S(2)}) async-start(bf16[8,2,1,128,128]{4,3,1,2,0:T(8,128)(2,1)} %stack.11), calls=%async_computation.4 | async-start | bytes 1048576 | tf_op jit(solution)/shard_map/all_to_all | solution.py:9
  459.2 86.0 %reduce-scatter.14.cloned.1.call-start = ((), (), s32[]{:S(2)}) async-start(), calls=%async_computation.7 | async-start | bytes 1179648 | tf_op jit(solution)/shard_map/reduce_scatter | solution.py:22
  474.1 3.2 copy-start.6
  474.1 4.7 copy-start.3
Sparse Core Ops, SparseCore 0:
  51.9 79.4 all-reduce.6
  167.8 77.2 all-reduce.8
  275.3 77.2 all-reduce.10
  388.9 63.2 reduce-scatter.11
  482.1 63.1 reduce-scatter.13
